TPU v7x, 128 devices: a whole 4x4x4 slice. The times are simulated.
128 devices in a mesh: dp: 32 (over x, y_lo, z), gz: 4 (over y_hi, core).
Axes of the slice: x: 4, y: 4 (y_hi: 2, y_lo: 2; y = y_hi * 2 + y_lo), z: 4, core: 2. Of those that a mesh axis runs over, the one named last changes fastest.
Arguments:
- field: bfloat16 [32, 16, 96, 9216], P('dp', None, 'gz'), may hold values from -6 to 6
- cotangent: bfloat16 [32, 16, 96, 9216], P('dp', None, 'gz'), may hold values from -36 to 36, as said below
- spec_weight: float32 [16, 16, 16, 256], P('gz'), may hold values from -1.5 to 1.5
- point_weight: bfloat16 [16, 16], replicated, may hold values from -1.5 to 1.5
- bias: float32 [16], replicated, may hold values from -3 to 3
Outputs:
- field_grad: bfloat16 [32, 16, 96, 9216], P('dp', None, 'gz')
- spectral_grad: float32 [16, 16, 16, 256], P('gz')
- point_grad: float32 [16, 16], replicated
- bias_grad: float32 [16], replicated
Inputs may be any that keep to these rules, and one draw needn't show every extreme that they name: `cotangent`: the gradient of the loss with respect to the layer's output.
All inputs are finite; a program needn't handle non-finite values.
Results may differ from a plain program's by a relative error of at most 0.007.
Values sent between devices are 32-bit elements; how exact they have to be, the bound alone decides.
No kernel may reach another device: no remote copies, remote signals or barrier semaphores. Data moves between devices by JAX's collectives and lax.ppermute only.
A program may use at most 192 MiB of HBM per device.

v0:
```python
import math
import jax
import jax.numpy as jnp
from jax import lax
from jax.sharding import PartitionSpec as P

N = 96
M = 16
root_half = 0.7071067811865476
density_norm = 0.3989422804014327


def basis_table(count_modes, length):
    mode_index = jnp.arange(count_modes, dtype=jnp.int32)
    half_count = count_modes // 2
    frequency = jnp.where(mode_index < half_count, mode_index, mode_index - half_count + 1)
    position = jnp.arange(length, dtype=jnp.int32)
    turns = frequency[:, None] * position[None, :] % length
    angle = turns.astype(jnp.float32) * (2.0 * math.pi / length)
    return jnp.where((mode_index < half_count)[:, None], jnp.cos(angle), jnp.sin(angle))


def kron_table(basis):
    outer = basis[:, None, :, None] * basis[None, :, None, :]
    return outer.reshape(M * M, N * N)


def gelu_slope(values):
    cumulative = 0.5 * (1.0 + lax.erf(values * root_half))
    return cumulative + values * jnp.exp(-0.5 * values * values) * density_norm


def shards(field, cotangent, spec_weight, point_weight, bias):
    highest = lax.Precision.HIGHEST
    samples_dev, channels, slab_rows, plane_cells = field.shape
    scale_fwd = (2.0 / N) ** 1.5
    scale_inv = (2.0 / M) ** 1.5
    basis = basis_table(M, N)
    kron = kron_table(basis)
    row_basis = lax.dynamic_slice_in_dim(basis, lax.axis_index("gz") * slab_rows, slab_rows, 1)
    contract_cells = (((1,), (1,)), ((), ()))

    def to_modes(values):
        flattened = values.reshape(samples_dev * channels * slab_rows, plane_cells).astype(
            jnp.float32
        )
        return lax.dot_general(flattened, kron, contract_cells, precision=highest).reshape(
            samples_dev, channels, slab_rows, M * M
        )

    def add_inverse(piece):
        piece_rows = piece.shape[0]
        inner = jnp.dot(
            piece.reshape(piece_rows * samples_dev * channels, M * M), kron, precision=highest
        )
        inner = inner.reshape(piece_rows, samples_dev, channels, plane_cells)
        return jnp.einsum("ax,asoz->soxz", row_basis, inner, precision=highest)

    line_modes = to_modes(field)
    rows_part = row_basis
    coefficients = lax.psum_scatter(
        scale_fwd * jnp.einsum("ax,scxp->ascp", rows_part, line_modes, precision=highest),
        "gz",
        scatter_dimension=0,
        tiled=True,
    )
    mixed_modes = jnp.einsum("asip,aiop->asop", coefficients, spec_weight, precision=highest)
    spectral = scale_inv * add_inverse(lax.all_gather(mixed_modes, "gz", axis=0, tiled=True))
    pre_act = (
        spectral
        + jnp.einsum("sixz,io->soxz", field, point_weight, preferred_element_type=jnp.float32)
        + bias[None, :, None, None]
    )
    grad_pre = (cotangent.astype(jnp.float32) * gelu_slope(pre_act)).astype(jnp.bfloat16)
    grad_line = to_modes(grad_pre)
    rows_part = row_basis
    grad_modes = lax.psum_scatter(
        scale_inv * jnp.einsum("ax,soxp->asop", rows_part, grad_line, precision=highest),
        "gz",
        scatter_dimension=0,
        tiled=True,
    )
    back_modes = jnp.einsum("aiop,asop->asip", spec_weight, grad_modes, precision=highest)
    field_spec = scale_fwd * add_inverse(lax.all_gather(back_modes, "gz", axis=0, tiled=True))
    field_grad = (
        field_spec
        + jnp.einsum("soxz,io->sixz", grad_pre, point_weight, preferred_element_type=jnp.float32)
    ).astype(jnp.bfloat16)
    local_point = jnp.einsum("sixz,soxz->io", field, grad_pre, preferred_element_type=jnp.float32)
    local_bias = jnp.sum(grad_pre, axis=(0, 2, 3), dtype=jnp.float32)
    total_point, total_bias = lax.psum((local_point, local_bias), ("dp", "gz"))
    local_spec = jnp.einsum("asip,asop->aiop", coefficients, grad_modes, precision=highest)
    grad_spec = lax.psum(local_spec, "dp")
    all_samples = samples_dev * lax.axis_size("dp")
    cell_norm = math.sqrt(all_samples * N * N * N)
    return (
        field_grad,
        grad_spec / math.sqrt(all_samples * N),
        total_point / cell_norm,
        total_bias / cell_norm,
    )


def solution(mesh):
    return jax.shard_map(
        shards,
        mesh=mesh,
        in_specs=(
            P("dp", None, "gz", None),
            P("dp", None, "gz", None),
            P("gz", None, None, None),
            P(),
            P(),
        ),
        out_specs=(P("dp", None, "gz", None), P("gz", None, None, None), P(), P()),
        check_vma=False,
    )
```

profile of v0, /device:TPU:0, one launch (start us, length us, event | category | flops | bytes accessed | tf_op | source)
XLA Modules:
  0.0 559.2 jit_solution(4819427986787261615)
XLA Ops:
  7.2 0.0 reduce-scatter.3.cloned.1.call-start
  7.3 0.1 sine_select_fusion
  7.4 6.2 %broadcast_multiply_fusion = f32[16,16,96,96]{3,2,1,0:T(8,128)} fusion(f32[16,96]{1,0:T(8,128)S(1)} %sine_select_fusion), kind=kLoop, calls=%fused_computation.12 | loop fusion | flops 2359296 | bytes 9443328 | tf_op jit(solution)/shard_map/mul | solution.py:24
  13.6 12.8 %mul.213 = f32[256,9216]{1,0:T(8,128)} reshape(f32[16,16,96,96]{3,2,1,0:T(8,128)} %broadcast_multiply_fusion) | data formatting | bytes 18874368 | tf_op jit(solution)/shard_map/mul | solution.py:24
  26.4 11.1 %convolution_bitcast_fusion = f32[384,256]{0,1:T(8,128)S(1)} fusion(f32[256,9216]{1,0:T(8,128)} %mul.213, bf16[384,9216]{1,0:T(8,128)(2,1)} %bitcast.98), kind=kOutput, calls=%fused_computation.20 | convolution fusion | flops 10871635968 | bytes 16908288 | tf_op jit(solution)/shard_map/dot_general | solution.py:47
  37.5 0.2 copy.31
  37.7 0.4 fusion.16
  38.1 0.9 copy.32
  39.0 0.0 reduce-scatter.5.cloned.1.call-start
  39.0 12.9 %reshape.211 = f32[256,9216,1]{1,0,2:T(8,128)} reshape(f32[16,16,96,96]{3,2,1,0:T(8,128)} %broadcast_multiply_fusion) | data formatting | bytes 18874368 | tf_op jit(solution)/shard_map/mul | solution.py:24
  51.9 11.7 %fusion.13 = f32[16,24,9216]{2,0,1:T(8,128)} fusion(bf16[16,24,9216]{2,1,0:T(8,128)(2,1)} %bitcast.99, bf16[16,16]{1,0:T(8,128)(2,1)S(1)} %copy-done), kind=kOutput, calls=%fused_computation.18 | convolution fusion | flops 113246208 | bytes 21234176 | tf_op jit(solution)/shard_map/sixz,io->soxz/dot_general | solution.py:71
  63.6 5.0 reduce-scatter.3.cloned.1.call-done
  68.6 1.1 multiply_reduce_fusion.1
  69.8 7.4 %all_gather.6 = f32[16,1,16,256]{3,2,1,0:T(8,128)S(1)} all-gather(f32[4,1,16,256]{3,2,1,0:T(8,128)S(1)} %bitcast.109), channel_id=1, replica_groups=mesh['dp'=32,'gz'=4] {'gz'}, dimensions={0}, use_global_device_ids=true | all-gather | bytes 327680 | tf_op jit(solution)/shard_map/all_gather | solution.py:68
  77.2 12.2 %fusion.24 = f32[16,16,9216]{2,0,1:T(8,128)S(1)} fusion(f32[256,9216,1]{1,0,2:T(8,128)} %reshape.211, f32[16,1,16,256]{3,2,1,0:T(8,128)S(1)} %all_gather.6), kind=kOutput, calls=%fused_computation.32 | convolution fusion | flops 7247757312 | bytes 19136512 | tf_op jit(solution)/shard_map/dot_general | solution.py:53
  89.4 25.9 %convert_reduce_fusion = (f32[16]{0:T(128)S(1)}, bf16[1,16,24,9216]{3,2,1,0:T(8,128)(2,1)}) fusion(f32[16]{0:T(128)S(1)} %copy-done.3, f32[16,24,9216]{2,0,1:T(8,128)} %fusion.13, f32[16,16,9216]{2,0,1:T(8,128)S(1)} %fusion.24, f32[16,96]{1,0:T(8,128)S(1)} %sine_select_fusion, s32[]{:T(128)S(6)} %select_n.65, bf16[1,16,24,9216]{3,2,1,0:T(8,128)(2,1)S(1)} %bitcast.112), kind=kOutput, calls=%fused_computation.11 | convolution fusion | flops 736100352 | bytes 37755012 | tf_op jit(solution)/shard_map/ax,asoz->soxz/dot_general | solution.py:57
  115.4 13.4 %fusion.47 = f32[16,24,256]{2,1,0:T(8,128)S(1)} fusion(f32[256,9216,1]{1,0,2:T(8,128)S(1)} %bitcast.97, bf16[1,16,24,9216]{3,2,1,0:T(8,128)(2,1)} %get-tuple-element.21), kind=kOutput, calls=%fused_computation.62 | convolution fusion | flops 10871635968 | bytes 16908288 | tf_op jit(solution)/shard_map/dot_general | solution.py:47
  128.9 17.8 %fusion.17 = f32[16,16]{0,1:T(8,128)S(1)} fusion(bf16[16,24,9216]{2,1,0:T(8,128)(2,1)S(1)} %bitcast.102, bf16[16,24,9216]{2,1,0:T(8,128)(2,1)} %bitcast.103), kind=kOutput, calls=%fused_computation.25 | convolution fusion | flops 113246208 | bytes 14156800 | tf_op jit(solution)/shard_map/sixz,soxz->io/dot_general | solution.py:89
  146.7 65.4 %all-reduce = (f32[16,16]{0,1:T(8,128)S(1)}, f32[16]{0:T(128)S(1)}) all-reduce(f32[16,16]{0,1:T(8,128)S(1)} %fusion.17, f32[16]{0:T(128)S(1)} %get-tuple-element.20), channel_id=1, replica_groups=mesh['dp'=32,'gz'=4] {'dp','gz'}, use_global_device_ids=true, to_apply=%region_3.4 | all-reduce | flops 272 | bytes 2176 | tf_op jit(solution)/shard_map/psum | solution.py:91
  212.2 0.7 copy.43
  212.8 0.5 broadcast_multiply_fusion.3
  213.4 0.4 fusion.15
  213.8 0.9 copy.37
  214.7 0.0 all-reduce.3.cloned.1.call-start
  214.7 16.0 %fusion.10 = f32[24,9216,16]{1,2,0:T(8,128)} fusion(bf16[16,24,9216]{2,1,0:T(8,128)(2,1)} %bitcast.104, bf16[16,16]{1,0:T(8,128)(2,1)S(1)} %copy-done), kind=kOutput, calls=%fused_computation.15 | convolution fusion | flops 113246208 | bytes 21234176 | tf_op jit(solution)/shard_map/soxz,io->sixz/dot_general | solution.py:87
  230.7 8.1 %reduce-scatter.5.cloned.1.call-done = f32[4,1,16,256]{3,2,1,0:T(8,128)} async-done(((f32[16,1,16,256]{3,2,1,0:T(8,128)}), f32[4,1,16,256]{3,2,1,0:T(8,128)}) %reduce-scatter.5.cloned.1.call-update) | async-done | bytes 65552 | tf_op jit(solution)/shard_map/reduce_scatter | solution.py:77
  238.8 2.1 multiply_bitcast_fusion
  240.9 7.3 %all_gather.7 = f32[16,1,16,256]{3,2,1,0:T(8,128)S(1)} all-gather(f32[4,1,16,256]{3,2,1,0:T(8,128)S(1)} %bitcast.108), channel_id=1, replica_groups=mesh['dp'=32,'gz'=4] {'gz'}, dimensions={0}, use_global_device_ids=true | all-gather | bytes 327680 | tf_op jit(solution)/shard_map/all_gather | solution.py:84
  248.2 12.2 %fusion.22 = f32[16,16,9216]{2,0,1:T(8,128)S(1)} fusion(f32[256,9216,1]{1,0,2:T(8,128)} %reshape.211, f32[16,1,16,256]{3,2,1,0:T(8,128)S(1)} %all_gather.7), kind=kOutput, calls=%fused_computation.30 | convolution fusion | flops 7247757312 | bytes 19136512 | tf_op jit(solution)/shard_map/dot_general | solution.py:53
  260.4 25.8 %fusion.6 = bf16[1,16,24,9216]{3,2,1,0:T(8,128)(2,1)} fusion(f32[24,9216,16]{1,2,0:T(8,128)} %fusion.10, f32[16,16,9216]{2,0,1:T(8,128)S(1)} %fusion.22, f32[16,96]{1,0:T(8,128)S(1)} %sine_select_fusion, s32[]{:T(128)S(6)} %select_n.65), kind=kOutput, calls=%fused_computation.8 | convolution fusion | flops 690094080 | bytes 30676996 | tf_op jit(solution)/shard_map/ax,asoz->soxz/dot_general | solution.py:57
  286.2 263.8 %all-reduce.3.cloned.1.call-done = f32[4,16,16,256]{3,2,1,0:T(8,128)} async-done(((f32[4,16,16,256]{3,2,1,0:T(8,128)}), f32[4,16,16,256]{3,2,1,0:T(8,128)}) %all-reduce.3.cloned.1.call-update) | async-done | bytes 1048592 | tf_op jit(solution)/shard_map/psum | solution.py:93
  550.0 2.3 broadcast_multiply_fusion.1
  (31 shorter events, 0.1 us)
Async XLA Ops:
  7.2 44.8 %copy-start = (bf16[16,16]{1,0:T(8,128)(2,1)S(1)}, bf16[16,16]{1,0:T(8,128)(2,1)}, u32[]{:S(2)}) copy-start(bf16[16,16]{1,0:T(8,128)(2,1)} %param.8) | copy-start | bytes 1540
  7.2 61.4 %reduce-scatter.3.cloned.1.call-start = ((), (), s32[]{:S(2)}) async-start(), calls=%async_computation.2 | async-start | bytes 327680 | tf_op jit(solution)/shard_map/reduce_scatter | solution.py:61
  39.0 199.8 %reduce-scatter.5.cloned.1.call-start = ((), (), s32[]{:S(2)}) async-start(), calls=%async_computation.3 | async-start | bytes 327680 | tf_op jit(solution)/shard_map/reduce_scatter | solution.py:77
  51.9 16.7 %copy-start.1 = (f32[4,16,16,256]{3,2,1,0:T(8,128)S(1)}, f32[4,16,16,256]{3,2,1,0:T(8,128)}, u32[]{:S(2)}) copy-start(f32[4,16,16,256]{3,2,1,0:T(8,128)} %param.7) | copy-start | bytes 3145732
  68.6 20.8 %slice-start.5 = ((s8[7077888]{0:T(1024)(128)(4,1)}), s8[4194304]{0:T(1024)(128)(4,1)S(1)}, s32[]{:S(2)}) async-start(s8[7077888]{0:T(1024)(128)(4,1)} %bitcast.111), calls=%async_computation.10 | async-start | bytes 8388608
  77.2 12.2 %slice-start.6 = ((s8[7077888]{0:T(1024)(128)(4,1)}), s8[2883584]{0:T(1024)(128)(4,1)S(1)}, s32[]{:S(2)}) async-start(s8[7077888]{0:T(1024)(128)(4,1)} %bitcast.111), calls=%async_computation.11 | async-start | bytes 5767168
  77.2 12.2 %copy-start.3 = (f32[16]{0:T(128)S(1)}, f32[16]{0:T(128)}, u32[]{:S(2)}) copy-start(f32[16]{0:T(128)} %param.9) | copy-start | bytes 196
  77.2 38.2 %slice-start = ((s8[9437184]{0:T(1024)(128)(4,1)}), s8[4194304]{0:T(1024)(128)(4,1)S(1)}, s32[]{:S(2)}) async-start(s8[9437184]{0:T(1024)(128)(4,1)} %bitcast.96), calls=%async_computation.5 | async-start | bytes 8388608
  89.4 26.0 %slice-start.1 = ((s8[9437184]{0:T(1024)(128)(4,1)}), s8[4194304]{0:T(1024)(128)(4,1)S(1)}, s32[]{:S(2)}) async-start(s8[9437184]{0:T(1024)(128)(4,1)} %bitcast.96), calls=%async_computation.6 | async-start | bytes 8388608
  89.4 26.0 %slice-start.2 = ((s8[9437184]{0:T(1024)(128)(4,1)}), s8[1048576]{0:T(1024)(128)(4,1)S(1)}, s32[]{:S(2)}) async-start(s8[9437184]{0:T(1024)(128)(4,1)} %bitcast.96), calls=%async_computation.7 | async-start | bytes 2097152
  115.4 13.5 %slice-start.3 = ((s8[7077888]{0:T(1024)(128)(4,1)}), s8[4194304]{0:T(1024)(128)(4,1)S(1)}, s32[]{:S(2)}) async-start(s8[7077888]{0:T(1024)(128)(4,1)} %bitcast.100), calls=%async_computation.8 | async-start | bytes 8388608
  115.4 13.4 %slice-start.4 = ((s8[7077888]{0:T(1024)(128)(4,1)}), s8[2883584]{0:T(1024)(128)(4,1)S(1)}, s32[]{:S(2)}) async-start(s8[7077888]{0:T(1024)(128)(4,1)} %bitcast.100), calls=%async_computation.9 | async-start | bytes 5767168
  214.7 24.1 %copy-start.2 = (f32[4,1,16,256]{3,2,1,0:T(8,128)S(1)}, f32[4,1,16,256]{3,2,1,0:T(8,128)}, u32[]{:S(2)}) copy-start(f32[4,1,16,256]{3,2,1,0:T(8,128)} %reduce-scatter.3.cloned.1.call-done) | copy-start | bytes 196612
  214.7 335.3 %all-reduce.3.cloned.1.call-start = ((), (), s32[]{:S(2)}) async-start(), calls=%async_computation.4 | async-start | bytes 2097152 | tf_op jit(solution)/shard_map/psum | solution.py:93
Sparse Core Ops, SparseCore 0:
  39.1 29.4 reduce-scatter.2
  214.8 23.9 reduce-scatter.4
  241.8 308.1 all-reduce.2
where the time goes:
time: 568 us; the launch traced here: 559 us
  waiting for transfers between devices  277 us (49%)
  matrix products  147 us (26%)
  blocking collectives  80.2 us (14%)
  local copies, waits for them, and re-layouts  28.3 us (5%)
  between operations  14.3 us (3%)
  other arithmetic  12.4 us (2%)
    psum x1, waiting for transfers between devices, shards(): grad_spec = lax.psum(local_spec, 'dp')  264 us
    psum x1, blocking collectives, shards(): total_point, total_bias = lax.psum((local_point, local_bias), ('dp', 'gz'))  65.4 us
    dot_general x2, matrix products, add_inverse(): return jnp.einsum('ax,asoz->soxz', row_basis, inner, precision=highest)  51.8 us
    mul x2, local copies, waits for them, and re-layouts, kron_table(): outer = basis[:, None, :, None] * basis[None, :, None, :]  25.7 us
    dot_general x2, matrix products, to_modes(): lax.dot_general(flattened, kron, contract_cells, precision=highest)  24.5 us
    dot_general x2, matrix products, add_inverse(): jnp.dot(piece.reshape(piece_rows * samples_dev * channels, M * M), kron,...  24.4 us
    dot_general x1, matrix products, shards(): jnp.einsum('sixz,soxz->io', field, grad_pre, preferred_element_type=jnp.f...  17.8 us
    dot_general x1, matrix products, shards(): jnp.einsum('soxz,io->sixz', grad_pre, point_weight, preferred_element_typ...  16 us
  transfers between devices with their start and end apart: 3, of which 3 were waited for; matrix products, arithmetic and copies ran while one was open for 14% of the time, Pallas kernels for 0%

commit v1 on v0

--- a/solution.py
+++ b/solution.py
@@ -8,6 +8,11 @@
 M = 16
 root_half = 0.7071067811865476
 density_norm = 0.3989422804014327
+
+
+def gather_and_add(x, axis):
+    parts = lax.all_gather(x, axis)
+    return jnp.sum(parts, axis=0)
 
 
 def basis_table(count_modes, length):
@@ -90,7 +95,7 @@
     local_bias = jnp.sum(grad_pre, axis=(0, 2, 3), dtype=jnp.float32)
     total_point, total_bias = lax.psum((local_point, local_bias), ("dp", "gz"))
     local_spec = jnp.einsum("asip,asop->aiop", coefficients, grad_modes, precision=highest)
-    grad_spec = lax.psum(local_spec, "dp")
+    grad_spec = gather_and_add(local_spec, "dp")
     all_samples = samples_dev * lax.axis_size("dp")
     cell_norm = math.sqrt(all_samples * N * N * N)
     return (

time: 568 us -> 660 us (1.16)
  blocking collectives: 80.2 us -> 412 us
  waiting for transfers between devices: 277 us -> 31.1 us
  other arithmetic: 12.4 us -> 23.4 us
    psum x1, blocking collectives: 65.4 us -> 387 us  [shards(): total_point, total_bias = lax.psum((local_point, local_bias), ('dp', 'gz'))]
    psum x1 -> x0, waiting for transfers between devices: 264 us -> none  [shards(): grad_spec = lax.psum(local_spec, 'dp')]
    reduce_scatter x1, waiting for transfers between devices: 8.07 us -> 26.1 us  [shards(): lax.psum_scatter(scale_inv * jnp.einsum('ax,soxp->asop', rows_part, grad_...]
    reduce_sum x0 -> x1, other arithmetic: none -> 12.3 us  [gather_and_add(): return jnp.sum(parts, axis=0)]
    all_gather x1, blocking collectives: 7.42 us -> 17.6 us  [shards(): lax.all_gather(mixed_modes, 'gz', axis=0, tiled=True)]
    dot_general x2, matrix products: 24.5 us -> 17.3 us  [to_modes(): lax.dot_general(flattened, kron, contract_cells, precision=highest)]
  transfers between devices with their start and end apart: 3 -> 3, of which waited for: 3 -> 2; matrix products, arithmetic and copies ran while one was open for 14% -> 15% of each run, Pallas kernels for 0% -> 0%
where the time goes in v1:
time: 660 us; the launch traced here: 650 us
  blocking collectives  412 us (62%)
  matrix products  141 us (21%)
  waiting for transfers between devices  31.1 us (5%)
  local copies, waits for them, and re-layouts  28.4 us (4%)
  other arithmetic  23.4 us (4%)
  between operations  14.3 us (2%)
    psum x1, blocking collectives, shards(): total_point, total_bias = lax.psum((local_point, local_bias), ('dp', 'gz'))  387 us
    dot_general x2, matrix products, add_inverse(): return jnp.einsum('ax,asoz->soxz', row_basis, inner, precision=highest)  50.9 us
    reduce_scatter x1, waiting for transfers between devices, shards(): lax.psum_scatter(scale_inv * jnp.einsum('ax,soxp->asop', rows_part, grad_...  26.1 us
    mul x2, local copies, waits for them, and re-layouts, kron_table(): outer = basis[:, None, :, None] * basis[None, :, None, :]  25.8 us
    dot_general x2, matrix products, add_inverse(): jnp.dot(piece.reshape(piece_rows * samples_dev * channels, M * M), kron,...  24.2 us
    dot_general x1, matrix products, shards(): jnp.einsum('sixz,soxz->io', field, grad_pre, preferred_element_type=jnp.f...  19.9 us
    all_gather x1, blocking collectives, shards(): lax.all_gather(mixed_modes, 'gz', axis=0, tiled=True)  17.6 us
    dot_general x2, matrix products, to_modes(): lax.dot_general(flattened, kron, contract_cells, precision=highest)  17.3 us
  transfers between devices with their start and end apart: 3, of which 2 were waited for; matrix products, arithmetic and copies ran while one was open for 15% of the time, Pallas kernels for 0%

profile of v1, /device:TPU:0, one launch (start us, length us, event | category | flops | bytes accessed | tf_op | source)
XLA Modules:
  0.0 650.4 jit_solution(12257270693698853265)
XLA Ops:
  7.2 0.0 reduce-scatter.3.cloned.1.call-start
  7.3 0.1 sine_select_fusion
  7.4 6.2 broadcast_multiply_fusion
  13.6 12.9 %mul.213 = f32[256,9216]{1,0:T(8,128)} reshape(f32[16,16,96,96]{3,2,1,0:T(8,128)} %broadcast_multiply_fusion) | data formatting | bytes 18874368 | tf_op jit(solution)/shard_map/mul | solution.py:29
  26.5 11.1 %convolution_bitcast_fusion = f32[384,256]{0,1:T(8,128)S(1)} fusion(f32[256,9216]{1,0:T(8,128)} %mul.213, bf16[384,9216]{1,0:T(8,128)(2,1)} %bitcast.100), kind=kOutput, calls=%fused_computation.20 | convolution fusion | flops 10871635968 | bytes 16908288 | tf_op jit(solution)/shard_map/dot_general | solution.py:52
  37.6 0.2 copy.31
  37.8 0.4 fusion.16
  38.2 0.9 copy.32
  39.1 0.0 reduce-scatter.5.cloned.1.call-start
  39.1 12.9 %reshape.212 = f32[256,9216,1]{1,0,2:T(8,128)} reshape(f32[16,16,96,96]{3,2,1,0:T(8,128)} %broadcast_multiply_fusion) | data formatting | bytes 18874368 | tf_op jit(solution)/shard_map/mul | solution.py:29
  52.0 11.7 %fusion.13 = f32[16,24,9216]{2,0,1:T(8,128)} fusion(bf16[16,24,9216]{2,1,0:T(8,128)(2,1)} %bitcast.101, bf16[16,16]{1,0:T(8,128)(2,1)S(1)} %copy-done), kind=kOutput, calls=%fused_computation.18 | convolution fusion | flops 113246208 | bytes 21234176 | tf_op jit(solution)/shard_map/sixz,io->soxz/dot_general | solution.py:76
  63.7 4.9 reduce-scatter.3.cloned.1.call-done
  68.7 1.0 multiply_reduce_fusion.1
  69.7 17.6 %all_gather.12 = f32[16,1,16,256]{3,2,1,0:T(8,128)S(1)} all-gather(f32[4,1,16,256]{3,2,1,0:T(8,128)S(1)} %bitcast.109), channel_id=1, replica_groups=mesh['dp'=32,'gz'=4] {'gz'}, dimensions={0}, use_global_device_ids=true | all-gather | bytes 327680 | tf_op jit(solution)/shard_map/all_gather | solution.py:73
  87.3 12.0 %fusion.24 = f32[16,16,9216]{2,0,1:T(8,128)S(1)} fusion(f32[256,9216,1]{1,0,2:T(8,128)} %reshape.212, f32[16,1,16,256]{3,2,1,0:T(8,128)S(1)} %all_gather.12), kind=kOutput, calls=%fused_computation.32 | convolution fusion | flops 7247757312 | bytes 19136512 | tf_op jit(solution)/shard_map/dot_general | solution.py:58
  99.3 25.1 %convert_reduce_fusion = (f32[16]{0:T(128)S(1)}, bf16[1,16,24,9216]{3,2,1,0:T(8,128)(2,1)S(1)}) fusion(f32[16]{0:T(128)S(1)} %copy-done.4, f32[16,24,9216]{2,0,1:T(8,128)} %fusion.13, f32[16,16,9216]{2,0,1:T(8,128)S(1)} %fusion.24, f32[16,96]{1,0:T(8,128)S(1)} %sine_select_fusion, s32[]{:T(128)S(6)} %select_n.65, bf16[1,16,24,9216]{3,2,1,0:T(8,128)(2,1)} %param.6), kind=kOutput, calls=%fused_computation.11 | convolution fusion | flops 736100352 | bytes 37755012 | tf_op jit(solution)/shard_map/ax,asoz->soxz/dot_general | solution.py:62
  124.5 6.2 fusion.47
  130.7 0.4 fusion.15
  131.1 0.9 copy.37
  132.0 0.4 all-gather.3.cloned.1.call-start
  132.4 26.1 %reduce-scatter.5.cloned.1.call-done = f32[4,1,16,256]{3,2,1,0:T(8,128)} async-done(((f32[16,1,16,256]{3,2,1,0:T(8,128)}), f32[4,1,16,256]{3,2,1,0:T(8,128)}) %reduce-scatter.5.cloned.1.call-update) | async-done | bytes 65552 | tf_op jit(solution)/shard_map/reduce_scatter | solution.py:82
  158.5 2.1 multiply_bitcast_fusion
  160.6 19.9 %fusion.17 = f32[16,16]{0,1:T(8,128)S(1)} fusion(bf16[16,24,9216]{2,1,0:T(8,128)(2,1)} %bitcast.102, bf16[16,24,9216]{2,1,0:T(8,128)(2,1)} %bitcast.103), kind=kOutput, calls=%fused_computation.25 | convolution fusion | flops 113246208 | bytes 14156800 | tf_op jit(solution)/shard_map/sixz,soxz->io/dot_general | solution.py:94
  180.5 387.2 %all-reduce = (f32[16,16]{0,1:T(8,128)S(1)}, f32[16]{0:T(128)S(1)}) all-reduce(f32[16,16]{0,1:T(8,128)S(1)} %fusion.17, f32[16]{0:T(128)S(1)} %get-tuple-element.20), channel_id=1, replica_groups=mesh['dp'=32,'gz'=4] {'dp','gz'}, use_global_device_ids=true, to_apply=%region_3.4 | all-reduce | flops 272 | bytes 2176 | tf_op jit(solution)/shard_map/psum | solution.py:96
  567.6 0.7 copy.43
  568.3 0.5 broadcast_multiply_fusion.3
  568.8 16.0 %fusion.10 = f32[24,9216,16]{1,2,0:T(8,128)} fusion(bf16[16,24,9216]{2,1,0:T(8,128)(2,1)} %bitcast.104, bf16[16,16]{1,0:T(8,128)(2,1)S(1)} %copy-done), kind=kOutput, calls=%fused_computation.15 | convolution fusion | flops 113246208 | bytes 21234176 | tf_op jit(solution)/shard_map/soxz,io->sixz/dot_general | solution.py:92
  584.8 7.3 %all_gather.13 = f32[16,1,16,256]{3,2,1,0:T(8,128)S(1)} all-gather(f32[4,1,16,256]{3,2,1,0:T(8,128)S(1)} %bitcast.108), channel_id=1, replica_groups=mesh['dp'=32,'gz'=4] {'gz'}, dimensions={0}, use_global_device_ids=true | all-gather | bytes 327680 | tf_op jit(solution)/shard_map/all_gather | solution.py:89
  592.1 12.2 %fusion.22 = f32[16,16,9216]{2,0,1:T(8,128)S(1)} fusion(f32[256,9216,1]{1,0,2:T(8,128)} %reshape.212, f32[16,1,16,256]{3,2,1,0:T(8,128)S(1)} %all_gather.13), kind=kOutput, calls=%fused_computation.30 | convolution fusion | flops 7247757312 | bytes 19136512 | tf_op jit(solution)/shard_map/dot_general | solution.py:58
  604.3 25.8 %fusion.6 = bf16[1,16,24,9216]{3,2,1,0:T(8,128)(2,1)} fusion(f32[24,9216,16]{1,2,0:T(8,128)} %fusion.10, f32[16,16,9216]{2,0,1:T(8,128)S(1)} %fusion.22, f32[16,96]{1,0:T(8,128)S(1)} %sine_select_fusion, s32[]{:T(128)S(6)} %select_n.65), kind=kOutput, calls=%fused_computation.8 | convolution fusion | flops 690094080 | bytes 30676996 | tf_op jit(solution)/shard_map/ax,asoz->soxz/dot_general | solution.py:62
  630.1 12.3 %reduce_sum.18 = f32[4,16,16,256]{3,2,1,0:T(8,128)S(1)} reduce(f32[32,4,16,16,256]{4,3,2,1,0:T(8,128)} %bitcast.99, f32[]{:T(128)} %constant.50.clone.1), dimensions={0}, to_apply=%region_2.3 | reduce | flops 8126464 | bytes 34603012 | tf_op jit(solution)/shard_map/reduce_sum | solution.py:15
  642.4 1.1 broadcast_multiply_fusion.1
  (24 shorter events, 0.1 us)
Async XLA Ops:
  7.2 44.9 %copy-start = (bf16[16,16]{1,0:T(8,128)(2,1)S(1)}, bf16[16,16]{1,0:T(8,128)(2,1)}, u32[]{:S(2)}) copy-start(bf16[16,16]{1,0:T(8,128)(2,1)} %param.8) | copy-start | bytes 1540
  7.2 61.5 %reduce-scatter.3.cloned.1.call-start = ((), (), s32[]{:S(2)}) async-start(), calls=%async_computation.2 | async-start | bytes 327680 | tf_op jit(solution)/shard_map/reduce_scatter | solution.py:66
  39.1 119.5 %reduce-scatter.5.cloned.1.call-start = ((), (), s32[]{:S(2)}) async-start(), calls=%async_computation.3 | async-start | bytes 327680 | tf_op jit(solution)/shard_map/reduce_scatter | solution.py:82
  52.0 16.7 %copy-start.2 = (f32[4,16,16,256]{3,2,1,0:T(8,128)S(1)}, f32[4,16,16,256]{3,2,1,0:T(8,128)}, u32[]{:S(2)}) copy-start(f32[4,16,16,256]{3,2,1,0:T(8,128)} %param.7) | copy-start | bytes 3145732
  87.3 12.0 %copy-start.4 = (f32[16]{0:T(128)S(1)}, f32[16]{0:T(128)}, u32[]{:S(2)}) copy-start(f32[16]{0:T(128)} %param.9) | copy-start | bytes 196
  87.3 37.2 %slice-start = ((s8[9437184]{0:T(1024)(128)(4,1)}), s8[4194304]{0:T(1024)(128)(4,1)S(1)}, s32[]{:S(2)}) async-start(s8[9437184]{0:T(1024)(128)(4,1)} %bitcast.97), calls=%async_computation.5 | async-start | bytes 8388608
  99.3 25.2 %slice-start.1 = ((s8[9437184]{0:T(1024)(128)(4,1)}), s8[4194304]{0:T(1024)(128)(4,1)S(1)}, s32[]{:S(2)}) async-start(s8[9437184]{0:T(1024)(128)(4,1)} %bitcast.97), calls=%async_computation.6 | async-start | bytes 8388608
  99.3 25.2 %slice-start.2 = ((s8[9437184]{0:T(1024)(128)(4,1)}), s8[1048576]{0:T(1024)(128)(4,1)S(1)}, s32[]{:S(2)}) async-start(s8[9437184]{0:T(1024)(128)(4,1)} %bitcast.97), calls=%async_computation.7 | async-start | bytes 2097152
  124.4 6.2 copy-start.1
  124.4 34.1 %copy-start.3 = (f32[4,1,16,256]{3,2,1,0:T(8,128)S(1)}, f32[4,1,16,256]{3,2,1,0:T(8,128)}, u32[]{:S(2)}) copy-start(f32[4,1,16,256]{3,2,1,0:T(8,128)} %reduce-scatter.3.cloned.1.call-done) | copy-start | bytes 196612
  132.0 498.1 %all-gather.3.cloned.1.call-start = ((), (), s32[]{:S(2)}) async-start(), calls=%async_computation.4 | async-start | bytes 34603008 | tf_op jit(solution)/shard_map/all_gather | solution.py:14
Sparse Core Ops, SparseCore 0:
  39.2 29.4 reduce-scatter.2
  132.1 26.3 reduce-scatter.4
  160.7 365.1 all-gather.2
